TPU v7x, 32 devices: a whole 2x2x4 slice. The times are simulated.
32 devices in a mesh: space: 4 (over y, core), vel: 8 (over z, x).
Axes of the slice: x: 2, y: 2, z: 4, core: 2. Of those that a mesh axis runs over, the one named last changes fastest.
Arguments:
- distribution: float32 [4, 256, 13824], P('space', None, 'vel'), may hold values from -6 to 6
- neighbours: int32 [4, 4], P('space'), may hold values from -1 to 3, as said below
- block_level: int32 [4], P('space'), may hold values from 0 to 2
- collide_mask: int32 [1024], P('space'), may hold values from 0 to 1, as said below
- gain_first: float32 [6, 13824], replicated, may hold values from -1.8 to 1.8
- gain_second: float32 [6, 13824], replicated, may hold values from -1.8 to 1.8
- loss_rates: float32 [13824], replicated, may hold values from 0.2 to 2
Outputs:
- distribution_next: float32 [4, 256, 13824], P('space', None, 'vel')
Inputs may be any that keep to these rules, and one draw needn't show every extreme that they name: `neighbours`: each entry is -1 or a block held by the same index of space as the block itself or by the index one below or one above (index s holds blocks s * 1 to (s + 1) - 1). `collide_mask`: the cells of one index of space (its 1 block) hold at most 128 ones, and some index holds exactly 128.
All inputs are finite; a program needn't handle non-finite values.
Results may differ from a plain program's by a relative error of at most 0.0003.
Values sent between devices are 32-bit elements; how exact they have to be, the bound alone decides.
A program may use at most 128 MiB of HBM per device.

v0:
```python
import jax
import jax.numpy as jnp
from jax import lax
from jax.sharding import PartitionSpec as P

BSIDE = 16
VDIM = 24
ACT = 128
weno_eps = 1e-06
courant = 0.2


def extended(cells, sides, width):
    for axis, dim in sides:
        count = lax.axis_size(axis)
        ends = count - 1
        head = lax.slice_in_dim(cells, 0, width, axis=dim)
        tail = lax.slice_in_dim(cells, cells.shape[dim] - width, cells.shape[dim], axis=dim)
        cells = jnp.concatenate(
            [
                lax.ppermute(tail, axis, [(i, (i + 1) % count) for i in range(ends)]),
                cells,
                lax.ppermute(head, axis, [((i + 1) % count, i) for i in range(ends)]),
            ],
            axis=dim,
        )
    return cells


def weno_value(minus_two, minus_one, middle, plus_one, plus_two):
    guess_low = (2.0 * minus_two - 7.0 * minus_one + 11.0 * middle) / 6.0
    guess_mid = (-minus_one + 5.0 * middle + 2.0 * plus_one) / 6.0
    guess_high = (2.0 * middle + 5.0 * plus_one - plus_two) / 6.0
    rough_low = (
        13.0 / 12.0 * (minus_two - 2.0 * minus_one + middle) ** 2
        + 0.25 * (minus_two - 4.0 * minus_one + 3.0 * middle) ** 2
    )
    rough_mid = (
        13.0 / 12.0 * (minus_one - 2.0 * middle + plus_one) ** 2
        + 0.25 * (minus_one - plus_one) ** 2
    )
    rough_high = (
        13.0 / 12.0 * (middle - 2.0 * plus_one + plus_two) ** 2
        + 0.25 * (3.0 * middle - 4.0 * plus_one + plus_two) ** 2
    )
    weight_low = 0.1 / (weno_eps + rough_low) ** 2
    weight_mid = 0.6 / (weno_eps + rough_mid) ** 2
    weight_high = 0.3 / (weno_eps + rough_high) ** 2
    return (weight_low * guess_low + weight_mid * guess_mid + weight_high * guess_high) / (
        weight_low + weight_mid + weight_high
    )


def edge_values(padded, along, cell_count):

    def shifted(offset):
        return lax.slice_in_dim(padded, offset, offset + cell_count + 1, axis=along)

    upwind_low = weno_value(shifted(0), shifted(1), shifted(2), shifted(3), shifted(4))
    upwind_high = weno_value(shifted(5), shifted(4), shifted(3), shifted(2), shifted(1))
    return (upwind_low, upwind_high)


def flux_change(padded, along, cell_count, velocity):
    from_low, from_high = edge_values(padded, along, cell_count)
    step_low = lax.slice_in_dim(from_low, 1, cell_count + 1, axis=along) - lax.slice_in_dim(
        from_low, 0, cell_count, axis=along
    )
    step_high = lax.slice_in_dim(from_high, 1, cell_count + 1, axis=along) - lax.slice_in_dim(
        from_high, 0, cell_count, axis=along
    )
    return jnp.maximum(velocity, 0.0) * step_low + jnp.minimum(velocity, 0.0) * step_high


def transport_rate(
    padded_first, padded_second, along, cell_count, speed_first, speed_second, courant_ratio
):
    change = flux_change(padded_first, along, cell_count, speed_first) + flux_change(
        padded_second, along + 1, cell_count, speed_second
    )
    return -courant_ratio * change


def grid_speeds(vel_start, vel_width, vdim):
    index = vel_start + jnp.arange(vel_width, dtype=jnp.int32)
    first_index = index // (vdim * vdim)
    second_index = index // vdim % vdim
    half = (vdim - 1) / 2.0
    return (
        (first_index.astype(jnp.float32) - half) / half,
        (second_index.astype(jnp.float32) - half) / half,
    )


def hartley(length):
    grid_index = jnp.arange(length, dtype=jnp.float32)
    angle_table = 2.0 * jnp.pi * grid_index[:, None] * grid_index[None, :] / length
    return (jnp.cos(angle_table) + jnp.sin(angle_table)) / jnp.sqrt(jnp.float32(length))


def hartley_cube(velocity_cube, hartley_table):
    highest = lax.Precision.HIGHEST
    row_count, vdim = (velocity_cube.shape[0], hartley_table.shape[0])
    current = velocity_cube
    for turn in range(3):
        mapped = jnp.dot(
            current.reshape(-1, vdim),
            hartley_table,
            precision=highest,
            preferred_element_type=jnp.float32,
        )
        current = jnp.transpose(mapped.reshape(row_count, vdim, vdim, vdim), (0, 3, 1, 2))
    return current


def collide(cell_rows, gain_first, gain_second, loss_rates, hartley_table):
    row_count = cell_rows.shape[0]
    vdim = hartley_table.shape[0]
    terms = gain_first.shape[0]
    velocity_cube = cell_rows.reshape(row_count, vdim, vdim, vdim)
    spectrum = hartley_cube(velocity_cube, hartley_table)
    multipliers = jnp.concatenate([gain_first, gain_second, loss_rates[None]], axis=0).reshape(
        -1, 1, vdim, vdim, vdim
    )
    stacked = (spectrum[None] * multipliers).reshape(-1, vdim, vdim, vdim)
    images = hartley_cube(stacked, hartley_table).reshape(
        2 * terms + 1, row_count, vdim, vdim, vdim
    )
    gain_total = jnp.sum(images[:terms] * images[terms : 2 * terms], axis=0)
    loss_part = images[2 * terms]
    return (gain_total - velocity_cube * loss_part).reshape(row_count, -1)


def shards(
    distribution, neighbours, block_level, collide_mask, gain_first, gain_second, loss_rates
):
    blocks, cell_count, vel_width = distribution.shape
    block_side = BSIDE
    density = distribution.reshape(blocks, block_side, block_side, vel_width)
    vel_start = lax.axis_index("vel") * vel_width
    speed_first, speed_second = grid_speeds(vel_start, vel_width, VDIM)
    courant_ratio = (courant * jnp.exp2(block_level.astype(jnp.float32)))[:, None, None, None]
    pool_start = (lax.axis_index("space") - 1) * blocks
    present = (neighbours >= 0).astype(jnp.float32)
    pool_index = jnp.where(neighbours >= 0, neighbours - pool_start, blocks)

    def local_rate(current):
        strip_size = 3 * block_side * vel_width
        packed = jnp.concatenate(
            [
                current[:, :3].reshape(blocks, -1),
                current[:, block_side - 3 :].reshape(blocks, -1),
                current[:, :, :3].reshape(blocks, -1),
                current[:, :, block_side - 3 :].reshape(blocks, -1),
            ],
            axis=1,
        )
        ghost_pool = extended(packed, (("space", 0),), blocks)

        def select_face(face_index, strip_index):
            strips = ghost_pool[:, strip_index * strip_size : (strip_index + 1) * strip_size]
            return strips[pool_index[:, face_index]] * present[:, face_index][:, None]

        ghost_west = select_face(0, 1).reshape(blocks, 3, block_side, vel_width)
        ghost_east = select_face(1, 0).reshape(blocks, 3, block_side, vel_width)
        ghost_south = select_face(2, 3).reshape(blocks, block_side, 3, vel_width)
        ghost_north = select_face(3, 2).reshape(blocks, block_side, 3, vel_width)
        padded_first = jnp.concatenate([ghost_west, current, ghost_east], axis=1)
        padded_second = jnp.concatenate([ghost_south, current, ghost_north], axis=2)
        return transport_rate(
            padded_first, padded_second, 1, block_side, speed_first, speed_second, courant_ratio
        )

    section_one = density + local_rate(density)
    section_two = 0.5 * density + 0.5 * (section_one + local_rate(section_one))
    hartley_table = hartley(VDIM)
    flat_cells = section_two.reshape(blocks * cell_count, vel_width)
    vel_parts = lax.axis_size("vel")
    capacity = ACT
    chosen = jnp.nonzero(collide_mask, size=capacity, fill_value=0)[0]
    filled = (jnp.arange(capacity) < jnp.sum(collide_mask)).astype(jnp.float32)
    slot_rows = flat_cells[chosen] * filled[:, None]
    collided = collide(
        lax.all_to_all(
            slot_rows.reshape(vel_parts, -1, vel_width),
            "vel",
            split_axis=0,
            concat_axis=2,
            tiled=True,
        )[0],
        gain_first,
        gain_second,
        loss_rates,
        hartley_table,
    )
    change = lax.all_to_all(collided[None], "vel", split_axis=2, concat_axis=0, tiled=True)
    change = change.reshape(capacity, vel_width) * filled[:, None]
    result = flat_cells.at[chosen].add(change)
    return result.reshape(blocks, cell_count, vel_width)


def solution(mesh):
    in_specs = (P("space", None, "vel"), P("space", None), P("space"), P("space"), P(), P(), P())
    out_specs = P("space", None, "vel")
    return jax.shard_map(shards, mesh=mesh, in_specs=in_specs, out_specs=out_specs, check_vma=False)
```

profile of v0, /device:TPU:1, one launch (start us, length us, event | category | flops | bytes accessed | tf_op | source)
XLA Modules:
  0.0 621.4 jit_solution(15037906959466052470)
XLA Ops:
  0.0 1.8 copy.96
  4.8 1.3 reshape.411
  9.2 1.9 collective-permute-start.1
  11.1 4.8 collective-permute-start
  25.5 3.8 collective-permute-done.1
  30.4 4.8 pad_maximum_fusion
  35.2 2.4 fusion.207
  37.6 2.4 fusion.150
  42.1 2.9 fusion.147
  46.1 2.9 fusion.148
  50.2 1.7 fusion.149
  53.1 1.2 fusion.210
  54.4 8.4 %fusion.111 = (f32[1,16,17,1728]{3,1,2,0:T(8,128)S(1)}, f32[1,16,17,1728]{3,1,2,0:T(8,128)S(1)}) fusion(f32[1,16,19,1728]{3,1,2,0:T(8,128)S(1)} %get-tuple-element.117, f32[1,16,19,1728]{3,1,2,0:T(8,128)S(1)} %copy_dynamic-update-slice_fusion.1), kind=kLoop, calls=%fused_computation.155 | loop fusion | flops 58281984 | bytes 15040512 | tf_op jit(solution)/shard_map/div | solution.py:49
  63.1 13.3 %fusion.60 = (f32[1,17,16,1728]{3,1,2,0:T(8,128)S(1)}, f32[1,17,16,1728]{3,1,2,0:T(8,128)S(1)}) fusion(f32[1,16,16,1728]{3,1,2,0:T(8,128)S(1)} %get-tuple-element.115, f32[1,3,16,1728]{3,1,2,0:T(4,128)S(1)} %copy-done.5, f32[1,19,16,1728]{3,1,2,0:T(8,128)S(1)} %copy_dynamic-update-slice_fusion), kind=kLoop, calls=%fused_computation.89 | loop fusion | flops 60162048 | bytes 11501568 | tf_op jit(solution)/shard_map/div | solution.py:49
  76.5 2.3 fusion.138
  80.4 1.3 reshape.416
  81.9 1.3 reshape.415
  88.7 1.9 collective-permute-start.3
  90.6 4.5 collective-permute-start.2
  95.8 2.3 scatter_custom_fusion
  100.5 8.2 %collective-permute-done.3 = f32[1,331776]{1,0:T(1,128)} collective-permute-done((f32[1,331776]{1,0:T(1,128)S(1)}, f32[1,331776]{1,0:T(1,128)}, u32[]{:S(2)}, u32[]{:S(2)}) %collective-permute-start.3) | collective-permute-done | bytes 1327136 | tf_op jit(solution)/shard_map/ppermute | solution.py:23
  109.8 5.4 pad_maximum_fusion.1
  115.2 2.0 fusion.206
  117.2 4.0 fusion.145
  125.4 5.3 fusion.143
  130.7 1.3 mul.984
  132.4 15.2 %fusion.89 = (f32[1,16,17,1728]{3,1,2,0:T(8,128)S(1)}, f32[1,16,17,1728]{3,1,2,0:T(8,128)S(1)}) fusion(f32[1,16,16,1728]{3,1,2,0:T(8,128)} %copy-done, f32[1,16,3,1728]{3,1,2,0:T(8,128)S(1)} %copy.112, f32[1,16,3,1728]{3,1,2,0:T(8,128)S(1)} %copy.113), kind=kLoop, calls=%fused_computation.128 | loop fusion | flops 63452160 | bytes 6193152 | tf_op jit(solution)/shard_map/div | solution.py:49
  147.7 13.8 %fusion.34 = (f32[1,17,16,1728]{3,1,2,0:T(8,128)S(1)}, f32[1,17,16,1728]{3,1,2,0:T(8,128)S(1)}) fusion(f32[1,16,16,1728]{3,1,2,0:T(8,128)S(1)} %copy-done.1, f32[1,3,16,1728]{3,1,2,0:T(4,128)S(1)} %copy-done.7, f32[1,3,16,1728]{3,1,2,0:T(4,128)S(1)} %copy-done.6), kind=kLoop, calls=%fused_computation.58 | loop fusion | flops 63452160 | bytes 6193152 | tf_op jit(solution)/shard_map/div | solution.py:49
  161.6 2.7 fusion.129
  167.4 5.5 all-to-all-start
  173.2 2.5 concatenate.78
  175.7 3.5 concatenate.79
  179.1 4.3 maximum_bitcast_fusion
  183.4 3.5 all-to-all-done
  187.8 1.7 copy.117
  189.5 1.4 reshape_squeeze.3
  190.9 3.1 dot_general.20
  194.0 6.0 fusion.159
  200.1 9.5 %fusion.71 = f32[16,24,24,24]{1,2,3,0:T(8,128)} fusion(f32[16,24,24,24]{3,2,1,0:T(8,128)S(1)} %fusion.159, f32[24]{0:T(128)S(1)} %iota_multiply_fusion), kind=kOutput, calls=%fused_computation.102 | convolution fusion | flops 63703296 | bytes 1769568 | tf_op jit(solution)/shard_map/dot_general | solution.py:106
  209.5 6.3 %copy.121 = f32[16,24,24,24]{3,2,1,0:T(8,128)} copy(f32[16,24,24,24]{1,2,3,0:T(8,128)} %fusion.71) | data formatting | bytes 1769472 | tf_op jit(solution)/shard_map/transpose | solution.py:112
  215.8 7.6 %convolution_bitcast_fusion = f32[16,24,24,24]{1,3,2,0:T(8,128)} fusion(f32[16,24,24,24]{3,2,1,0:T(8,128)} %copy.121, f32[24]{0:T(128)S(1)} %iota_multiply_fusion), kind=kOutput, calls=%fused_computation.103 | convolution fusion | flops 63703296 | bytes 1769568 | tf_op jit(solution)/shard_map/dot_general | solution.py:106
  223.4 6.2 copy.123
  229.6 22.1 %broadcast_multiply_fusion = f32[13,16,24,24,24]{4,3,2,1,0:T(8,128)} fusion(f32[13,24,24,24]{3,2,1,0:T(8,128)} %maximum_bitcast_fusion, f32[16,24,24,24]{3,2,1,0:T(8,128)} %copy.123), kind=kLoop, calls=%fused_computation.5 | loop fusion | flops 2875392 | bytes 13105152 | tf_op jit(solution)/shard_map/mul | solution.py:125
  251.7 110.7 %fusion.12 = f32[208,24,24,24]{0,1,3,2:T(8,128)} fusion(f32[208,24,24,24]{3,2,1,0:T(8,128)} %bitcast.86, f32[24]{0:T(128)S(1)} %iota_multiply_fusion), kind=kOutput, calls=%fused_computation.12 | convolution fusion | flops 828115200 | bytes 23003232 | tf_op jit(solution)/shard_map/dot_general | solution.py:106
  362.4 21.1 %fusion.6 = f32[208,24,24,24]{0,1,3,2:T(8,128)S(1)} fusion(f32[208,24,24,24]{0,1,3,2:T(8,128)} %fusion.12, f32[24]{0:T(128)S(1)} %iota_multiply_fusion), kind=kOutput, calls=%fused_computation.10 | convolution fusion | flops 828115200 | bytes 23003232 | tf_op jit(solution)/shard_map/dot_general | solution.py:106
  383.6 19.6 %fusion.9 = f32[208,24,24,24]{0,1,3,2:T(8,128)} fusion(f32[208,24,24,24]{0,1,3,2:T(8,128)S(1)} %fusion.6, f32[24]{0:T(128)S(1)} %iota_multiply_fusion), kind=kOutput, calls=%fused_computation.11 | convolution fusion | flops 828115200 | bytes 23003232 | tf_op jit(solution)/shard_map/dot_general | solution.py:106
  403.2 11.8 %slice_multiply_fusion = f32[96,24,24,24]{0,1,3,2:T(8,128)} fusion(f32[208,24,24,24]{0,1,3,2:T(8,128)} %fusion.9), kind=kLoop, calls=%fused_computation.13 | loop fusion | flops 1327104 | bytes 15925248 | tf_op jit(solution)/shard_map/mul | solution.py:129
  415.0 7.7 %slice.449 = f32[16,24,24,24]{0,1,3,2:T(8,128)} slice(f32[208,24,24,24]{0,1,3,2:T(8,128)} %fusion.9), slice={[192:208], [0:24], [0:24], [0:24]} | slice | bytes 1769472 | tf_op jit(solution)/shard_map/slice | solution.py:130
  422.7 9.5 %copy.129 = f32[16,24,24,24]{3,2,1,0:T(8,128)} copy(f32[16,24,24,24]{0,1,3,2:T(8,128)} %slice.449) | data formatting | bytes 1769472 | tf_op jit(solution)/shard_map/slice | solution.py:130
  432.2 5.5 squeeze.23
  437.7 23.0 %copy.127 = f32[96,24,24,24]{3,2,1,0:T(8,128)} copy(f32[96,24,24,24]{0,1,3,2:T(8,128)} %slice_multiply_fusion) | data formatting | bytes 10616832 | tf_op jit(solution)/shard_map/mul | solution.py:129
  460.7 13.0 %reduce_sum.31 = f32[16,24,24,24]{3,2,1,0:T(8,128)} reduce(f32[6,16,24,24,24]{4,3,2,1,0:T(8,128)} %bitcast.90, f32[]{:T(128)} %constant.144.clone.1), dimensions={0}, to_apply=%region_6.7 | reduce | flops 1105920 | bytes 6193156 | tf_op jit(solution)/shard_map/reduce_sum | solution.py:129
  473.8 5.4 reduce_sum.32
  479.2 2.5 multiply_subtract_fusion.8
  481.6 13.4 %copy.130 = f32[1,16,13824]{1,0,2:T(1,128)} copy(f32[1,16,13824]{2,1,0:T(8,128)} %multiply_subtract_fusion.8) | data formatting | bytes 1769472 | tf_op jit(solution)/shard_map/sub | solution.py:131
  495.5 66.0 %reduce.36 = f32[13824,16]{1,0:T(8,128)} reduce(f32[13824,1,16]{2,1,0:T(1,128)} %bitcast.96, f32[]{:T(128)} %broadcast.820), dimensions={1}, to_apply=%bitcast.82.reduce_sub_computation | reduce | bytes 1769476
  561.5 5.8 reshape.653
  567.3 4.0 all-to-all-start.1
  571.9 16.0 %all-to-all-done.1 = f32[8,1,27648]{2,1,0:T(1,128)S(1)} async-done(((f32[8,1,27648]{2,1,0:T(1,128)}), f32[8,1,27648]{2,1,0:T(1,128)S(1)}, u32[]{:S(2)}, u32[]{:S(2)}) %all-to-all-start.1) | async-done | bytes 884768 | tf_op jit(solution)/shard_map/all_to_all | solution.py:196
  587.9 3.9 reduce.37
  591.8 19.7 %reshape.654 = f32[13824,1,16]{2,1,0:T(1,128)} reshape(f32[8,27648]{1,0:T(8,128)} %reduce.37) | data formatting | bytes 1769472
  611.5 4.8 copy.142
  616.9 2.7 scatter_fusion
  619.6 1.7 copy.133
  (115 shorter events, 36.6 us)
Async XLA Ops:
  4.2 11.7 %copy-start.22 = (s32[1,4]{1,0:T(1,128)S(1)}, s32[1,4]{1,0:T(1,128)}, u32[]{:S(2)}) copy-start(s32[1,4]{1,0:T(1,128)} %param.8) | copy-start | bytes 52
  9.2 20.1 %collective-permute-start.1 = (f32[1,331776]{1,0:T(1,128)S(1)}, f32[1,331776]{1,0:T(1,128)}, u32[]{:S(2)}, u32[]{:S(2)}) collective-permute-start(f32[1,331776]{1,0:T(1,128)S(1)} %constant_dynamic-update-slice_fusion), channel_id=1, source_target_pairs={{8,0},{16,8},{24,16},{9,1},{17,9},{25,17},{10,2},{18,10},{26,18},{... | collective-permute-start | bytes 3981320 | tf_op jit(solution)/shard_map/ppermute | solution.py:23
  11.1 19.2 %collective-permute-start = (f32[1,331776]{1,0:T(1,128)S(1)}, f32[1,331776]{1,0:T(1,128)}, u32[]{:S(2)}, u32[]{:S(2)}) collective-permute-start(f32[1,331776]{1,0:T(1,128)S(1)} %constant_dynamic-update-slice_fusion), channel_id=1, source_target_pairs={{0,8},{8,16},{16,24},{1,9},{9,17},{17,25},{2,10},{10,18},{18,26},{... | collective-permute-start | bytes 3981320 | tf_op jit(solution)/shard_map/ppermute | solution.py:21
  24.7 51.7 %copy-start.10 = (f32[1728]{0:T(1024)}, f32[1728]{0:T(1024)S(1)}, u32[]{:S(2)}) copy-start(f32[1728]{0:T(1024)S(1)} %broadcast_minimum_fusion.1) | copy-start | bytes 20740
  24.7 51.7 %copy-start.12 = (f32[1728]{0:T(1024)}, f32[1728]{0:T(1024)S(1)}, u32[]{:S(2)}) copy-start(f32[1728]{0:T(1024)S(1)} %broadcast_minimum_fusion) | copy-start | bytes 20740
  24.8 51.7 %copy-start.14 = (f32[1728]{0:T(1024)}, f32[1728]{0:T(1024)S(1)}, u32[]{:S(2)}) copy-start(f32[1728]{0:T(1024)S(1)} %broadcast_maximum_fusion) | copy-start | bytes 20740
  24.8 51.6 %copy-start.16 = (f32[1728]{0:T(1024)}, f32[1728]{0:T(1024)S(1)}, u32[]{:S(2)}) copy-start(f32[1728]{0:T(1024)S(1)} %broadcast_maximum_fusion.1) | copy-start | bytes 20740
  53.0 1.2 copy-start.4
  54.4 8.8 %copy-start.5 = (f32[1,3,16,1728]{3,1,2,0:T(4,128)S(1)}, f32[1,3,16,1728]{3,1,2,0:T(4,128)}, u32[]{:S(2)}) copy-start(f32[1,3,16,1728]{3,1,2,0:T(4,128)} %copy.97) | copy-start | bytes 995332
  78.8 1.3 copy-start
  83.3 5.4 copy-start.8
  84.4 10.7 %copy-start.21 = (s32[256]{0:T(256)S(1)}, s32[256]{0:T(256)}, u32[]{:S(2)}) copy-start(s32[256]{0:T(256)} %param.10) | copy-start | bytes 3076
  88.7 20.1 %collective-permute-start.3 = (f32[1,331776]{1,0:T(1,128)S(1)}, f32[1,331776]{1,0:T(1,128)}, u32[]{:S(2)}, u32[]{:S(2)}) collective-permute-start(f32[1,331776]{1,0:T(1,128)S(1)} %constant_dynamic-update-slice_fusion.7), channel_id=1, source_target_pairs={{8,0},{16,8},{24,16},{9,1},{17,9},{25,17},{10,2},{18,10},{26,18},{... | collective-permute-start | bytes 3981320 | tf_op jit(solution)/shard_map/ppermute | solution.py:23
  90.6 19.2 %collective-permute-start.2 = (f32[1,331776]{1,0:T(1,128)S(1)}, f32[1,331776]{1,0:T(1,128)}, u32[]{:S(2)}, u32[]{:S(2)}) collective-permute-start(f32[1,331776]{1,0:T(1,128)S(1)} %constant_dynamic-update-slice_fusion.7), channel_id=1, source_target_pairs={{0,8},{8,16},{16,24},{1,9},{9,17},{17,25},{2,10},{10,18},{18,26},{... | collective-permute-start | bytes 3981320 | tf_op jit(solution)/shard_map/ppermute | solution.py:21
  100.5 14.7 %copy-start.19 = (s32[128]{0:T(128)}, s32[128]{0:T(128)S(1)}, u32[]{:S(2)}) copy-start(s32[128]{0:T(128)S(1)} %fusion.153) | copy-start | bytes 1540
  132.4 15.2 %copy-start.1 = (f32[1,16,16,1728]{3,1,2,0:T(8,128)S(1)}, f32[1,16,16,1728]{3,1,2,0:T(8,128)}, u32[]{:S(2)}) copy-start(f32[1,16,16,1728]{3,1,2,0:T(8,128)} %copy-done) | copy-start | bytes 5308420
  132.4 15.2 %copy-start.6 = (f32[1,3,16,1728]{3,1,2,0:T(4,128)S(1)}, f32[1,3,16,1728]{3,1,2,0:T(4,128)}, u32[]{:S(2)}) copy-start(f32[1,3,16,1728]{3,1,2,0:T(4,128)} %copy.111) | copy-start | bytes 995332
  132.4 15.2 %copy-start.7 = (f32[1,3,16,1728]{3,1,2,0:T(4,128)S(1)}, f32[1,3,16,1728]{3,1,2,0:T(4,128)}, u32[]{:S(2)}) copy-start(f32[1,3,16,1728]{3,1,2,0:T(4,128)} %copy.110) | copy-start | bytes 995332
  147.7 13.9 %copy-start.11 = (f32[1728]{0:T(1024)S(1)}, f32[1728]{0:T(1024)}, u32[]{:S(2)}) copy-start(f32[1728]{0:T(1024)} %copy-done.10) | copy-start | bytes 20740
  147.7 13.9 %copy-start.13 = (f32[1728]{0:T(1024)S(1)}, f32[1728]{0:T(1024)}, u32[]{:S(2)}) copy-start(f32[1728]{0:T(1024)} %copy-done.12) | copy-start | bytes 20740
  147.7 13.9 %copy-start.15 = (f32[1728]{0:T(1024)S(1)}, f32[1728]{0:T(1024)}, u32[]{:S(2)}) copy-start(f32[1728]{0:T(1024)} %copy-done.14) | copy-start | bytes 20740
  147.7 13.9 %copy-start.17 = (f32[1728]{0:T(1024)S(1)}, f32[1728]{0:T(1024)}, u32[]{:S(2)}) copy-start(f32[1728]{0:T(1024)} %copy-done.16) | copy-start | bytes 20740
  166.3 6.6 %copy-start.18 = (f32[13824]{0:T(1024)S(1)}, f32[13824]{0:T(1024)}, u32[]{:S(2)}) copy-start(f32[13824]{0:T(1024)} %param.13) | copy-start | bytes 165892
  166.4 6.8 %copy-start.9 = (f32[6,13824]{1,0:T(8,128)S(1)}, f32[6,13824]{1,0:T(8,128)}, u32[]{:S(2)}) copy-start(f32[6,13824]{1,0:T(8,128)} %param.11) | copy-start | bytes 995332
  167.4 19.5 %all-to-all-start = ((f32[8,16,1728]{2,1,0:T(8,128)}), f32[8,16,1728]{2,1,0:T(8,128)S(1)}, u32[]{:S(2)}, u32[]{:S(2)}) async-start(f32[8,16,1728]{2,1,0:T(8,128)} %broadcast_multiply_fusion.1), calls=%async_computation | async-start | bytes 1835008 | tf_op jit(solution)/shard_map/all_to_all | solution.py:184
  186.9 0.9 copy-start.2
  473.8 5.4 copy-start.3
  567.3 20.7 %all-to-all-start.1 = ((f32[8,1,27648]{2,1,0:T(1,128)}), f32[8,1,27648]{2,1,0:T(1,128)S(1)}, u32[]{:S(2)}, u32[]{:S(2)}) async-start(f32[8,1,27648]{2,1,0:T(1,128)} %reshape.653), calls=%async_computation.1 | async-start | bytes 1769472 | tf_op jit(solution)/shard_map/all_to_all | solution.py:196
  616.3 0.6 copy-start.20
where the time goes:
time: 627 us; the launch traced here: 621 us
  other arithmetic  218 us (35%)
  matrix products  175 us (28%)
  local copies, waits for them, and re-layouts  163 us (26%)
  waiting for transfers between devices  33.7 us (5%)
  starting transfers between devices  22.6 us (4%)
  between operations  8.98 us (1%)
    dot_general x6, matrix products, hartley_cube(): jnp.dot(current.reshape(-1, vdim), hartley_table, precision=highest, pref...  175 us
    unnamed x1, other arithmetic  66 us
    div x4, other arithmetic, weno_value(): (weight_low * guess_low + weight_mid * guess_mid + weight_high * guess_hi...  50.8 us
    unnamed x57, local copies, waits for them, and re-layouts  37.3 us
    mul x2, other arithmetic, collide(): stacked = (spectrum[None] * multipliers).reshape(-1, vdim, vdim, vdim)  26.4 us
    mul x1, local copies, waits for them, and re-layouts, collide(): gain_total = jnp.sum(images[:terms] * images[terms:2 * terms], axis=0)  23 us
    mul x6, other arithmetic, select_face(): return strips[pool_index[:, face_index]] * present[:, face_index][:, None]  19.2 us
    slice x2, local copies, waits for them, and re-layouts, collide(): loss_part = images[2 * terms]  17.2 us
  transfers between devices with their start and end apart: 6, of which 6 were waited for; matrix products, arithmetic and copies ran while one was open for 3% of the time, Pallas kernels for 0%

commit v1 on v0

--- a/solution.py
+++ b/solution.py
@@ -193,7 +193,12 @@
         loss_rates,
         hartley_table,
     )
-    change = lax.all_to_all(collided[None], "vel", split_axis=2, concat_axis=0, tiled=True)
+    inner_x = collided[None]
+    w2 = lax.axis_size("vel")
+    m_next = jnp.split(inner_x, w2, axis=2)
+    w_next = jnp.stack(m_next)
+    shaped = lax.all_to_all(w_next, "vel", split_axis=0, concat_axis=0)
+    change = jnp.concatenate(shaped, axis=0)
     change = change.reshape(capacity, vel_width) * filled[:, None]
     result = flat_cells.at[chosen].add(change)
     return result.reshape(blocks, cell_count, vel_width)

time: 627 us -> 518 us (0.83)
  other arithmetic: 218 us -> 149 us
  local copies, waits for them, and re-layouts: 163 us -> 124 us
    unnamed x1 -> x0, other arithmetic: 66 us -> none
    unnamed x57, local copies, waits for them, and re-layouts: 37.3 us -> 16 us
    sub x1 -> x0, local copies, waits for them, and re-layouts: 13.4 us -> none  [collide(): return (gain_total - velocity_cube * loss_part).reshape(row_count, -1)]
where the time goes in v1:
time: 518 us; the launch traced here: 513 us
  matrix products  175 us (34%)
  other arithmetic  149 us (29%)
  local copies, waits for them, and re-layouts  124 us (24%)
  waiting for transfers between devices  34.2 us (7%)
  starting transfers between devices  22.5 us (4%)
  between operations  8.98 us (2%)
    dot_general x6, matrix products, hartley_cube(): jnp.dot(current.reshape(-1, vdim), hartley_table, precision=highest, pref...  175 us
    div x4, other arithmetic, weno_value(): (weight_low * guess_low + weight_mid * guess_mid + weight_high * guess_hi...  50.6 us
    mul x2, other arithmetic, collide(): stacked = (spectrum[None] * multipliers).reshape(-1, vdim, vdim, vdim)  26.4 us
    mul x1, local copies, waits for them, and re-layouts, collide(): gain_total = jnp.sum(images[:terms] * images[terms:2 * terms], axis=0)  23 us
    mul x6, other arithmetic, select_face(): return strips[pool_index[:, face_index]] * present[:, face_index][:, None]  19.2 us
    slice x2, local copies, waits for them, and re-layouts, collide(): loss_part = images[2 * terms]  17.2 us
    all_to_all x1, waiting for transfers between devices, shards(): shaped = lax.all_to_all(w_next, 'vel', split_axis=0, concat_axis=0)  16.8 us
    unnamed x57, local copies, waits for them, and re-layouts  16 us
  transfers between devices with their start and end apart: 6, of which 6 were waited for; matrix products, arithmetic and copies ran while one was open for 3% of the time, Pallas kernels for 0%

profile of v1, /device:TPU:1, one launch (start us, length us, event | category | flops | bytes accessed | tf_op | source)
XLA Modules:
  0.0 513.3 jit_solution(9908777567664551467)
XLA Ops:
  0.0 1.8 copy.93
  2.0 1.1 reshape.406
  3.1 1.1 reshape.405
  4.8 1.3 reshape.407
  9.2 1.9 collective-permute-start.1
  11.1 5.0 collective-permute-start
  25.8 3.5 collective-permute-done.1
  30.4 4.8 pad_maximum_fusion
  35.2 2.4 fusion.215
  37.6 2.4 fusion.150
  42.1 2.9 fusion.147
  46.1 2.9 fusion.148
  50.2 1.7 fusion.149
  52.0 1.1 copy_dynamic-update-slice_fusion.2
  53.1 1.2 fusion.218
  54.4 8.4 %fusion.111 = (f32[1,16,17,1728]{3,1,2,0:T(8,128)S(1)}, f32[1,16,17,1728]{3,1,2,0:T(8,128)S(1)}) fusion(f32[1,16,19,1728]{3,1,2,0:T(8,128)S(1)} %get-tuple-element.117, f32[1,16,19,1728]{3,1,2,0:T(8,128)S(1)} %copy_dynamic-update-slice_fusion.1), kind=kLoop, calls=%fused_computation.155 | loop fusion | flops 58281984 | bytes 15040512 | tf_op jit(solution)/shard_map/div | solution.py:49
  63.1 13.2 %fusion.60 = (f32[1,17,16,1728]{3,1,2,0:T(8,128)S(1)}, f32[1,17,16,1728]{3,1,2,0:T(8,128)S(1)}) fusion(f32[1,16,16,1728]{3,1,2,0:T(8,128)S(1)} %get-tuple-element.115, f32[1,3,16,1728]{3,1,2,0:T(4,128)S(1)} %copy-done.5, f32[1,19,16,1728]{3,1,2,0:T(8,128)S(1)} %copy_dynamic-update-slice_fusion), kind=kLoop, calls=%fused_computation.89 | loop fusion | flops 60162048 | bytes 11501568 | tf_op jit(solution)/shard_map/div | solution.py:49
  76.3 2.3 fusion.138
  78.7 1.2 copy-done
  80.3 1.3 reshape.412
  81.8 1.3 reshape.411
  83.2 1.1 reshape.410
  84.4 1.1 reshape.409
  88.6 1.9 collective-permute-start.3
  90.5 4.5 collective-permute-start.2
  95.7 2.3 scatter_custom_fusion
  100.3 8.3 %collective-permute-done.3 = f32[1,331776]{1,0:T(1,128)} collective-permute-done((f32[1,331776]{1,0:T(1,128)S(1)}, f32[1,331776]{1,0:T(1,128)}, u32[]{:S(2)}, u32[]{:S(2)}) %collective-permute-start.3) | collective-permute-done | bytes 1327136 | tf_op jit(solution)/shard_map/ppermute | solution.py:23
  109.7 5.0 pad_maximum_fusion.1
  114.8 2.0 fusion.214
  116.8 4.0 fusion.145
  124.9 5.3 %fusion.143 = (f32[82944]{0:T(1024)}, f32[82944]{0:T(1024)S(1)}) fusion(f32[3,82944]{1,0:T(4,128)S(1)} %get-tuple-element.96, s32[]{:T(128)} %bitcast.12, f32[]{:T(128)} %bitcast.13, f32[]{:T(128)} %bitcast.10, f32[3,82944]{1,0:T(4,128)} %get-tuple-element.97, s32[]{:T(128)} %bitcast.9), kind=kLoop, calls=%fused_computation.204 | loop fusion | flops 165888 | bytes 1327120 | tf_op jit(solution)/shard_map/mul | solution.py:162
  130.2 1.3 mul.984
  132.0 15.2 %fusion.89 = (f32[1,16,17,1728]{3,1,2,0:T(8,128)S(1)}, f32[1,16,17,1728]{3,1,2,0:T(8,128)S(1)}) fusion(f32[1,16,16,1728]{3,1,2,0:T(8,128)} %copy-done, f32[1,16,3,1728]{3,1,2,0:T(8,128)S(1)} %copy.109, f32[1,16,3,1728]{3,1,2,0:T(8,128)S(1)} %copy.110), kind=kLoop, calls=%fused_computation.128 | loop fusion | flops 63452160 | bytes 6193152 | tf_op jit(solution)/shard_map/div | solution.py:49
  147.3 13.8 %fusion.34 = (f32[1,17,16,1728]{3,1,2,0:T(8,128)S(1)}, f32[1,17,16,1728]{3,1,2,0:T(8,128)S(1)}) fusion(f32[1,16,16,1728]{3,1,2,0:T(8,128)S(1)} %copy-done.1, f32[1,3,16,1728]{3,1,2,0:T(4,128)S(1)} %copy-done.7, f32[1,3,16,1728]{3,1,2,0:T(4,128)S(1)} %copy-done.6), kind=kLoop, calls=%fused_computation.58 | loop fusion | flops 63452160 | bytes 6193152 | tf_op jit(solution)/shard_map/div | solution.py:49
  161.2 2.9 fusion.129
  167.3 5.5 %all-to-all-start = ((f32[8,16,1728]{2,1,0:T(8,128)}), f32[8,16,1728]{2,1,0:T(8,128)S(1)}, u32[]{:S(2)}, u32[]{:S(2)}) async-start(f32[8,16,1728]{2,1,0:T(8,128)} %broadcast_multiply_fusion.1), calls=%async_computation | async-start | bytes 1835008 | tf_op jit(solution)/shard_map/all_to_all | solution.py:184
  173.0 2.5 concatenate.78
  175.5 3.5 concatenate.79
  179.0 4.3 maximum_bitcast_fusion
  183.2 3.5 all-to-all-done
  187.6 1.7 copy.114
  189.3 1.4 reshape_squeeze.3
  190.7 3.1 dot_general.20
  193.8 6.1 %fusion.167 = f32[16,24,24,24]{3,2,1,0:T(8,128)S(1)} fusion(f32[16,24,24,24]{3,2,1,0:T(8,128)} %dot_general.20, f32[24]{0:T(128)S(1)} %iota_multiply_fusion), kind=kOutput, calls=%fused_computation.259 | convolution fusion | flops 63703296 | bytes 1769568 | tf_op jit(solution)/shard_map/dot_general | solution.py:106
  199.9 9.5 %fusion.71 = f32[16,24,24,24]{1,2,3,0:T(8,128)} fusion(f32[16,24,24,24]{3,2,1,0:T(8,128)S(1)} %fusion.167, f32[24]{0:T(128)S(1)} %iota_multiply_fusion), kind=kOutput, calls=%fused_computation.102 | convolution fusion | flops 63703296 | bytes 1769568 | tf_op jit(solution)/shard_map/dot_general | solution.py:106
  209.3 6.3 %copy.118 = f32[16,24,24,24]{3,2,1,0:T(8,128)} copy(f32[16,24,24,24]{1,2,3,0:T(8,128)} %fusion.71) | data formatting | bytes 1769472 | tf_op jit(solution)/shard_map/transpose | solution.py:112
  215.6 7.4 %convolution_bitcast_fusion = f32[16,24,24,24]{1,3,2,0:T(8,128)} fusion(f32[16,24,24,24]{3,2,1,0:T(8,128)} %copy.118, f32[24]{0:T(128)S(1)} %iota_multiply_fusion), kind=kOutput, calls=%fused_computation.103 | convolution fusion | flops 63703296 | bytes 1769568 | tf_op jit(solution)/shard_map/dot_general | solution.py:106
  223.0 6.2 %copy.120 = f32[16,24,24,24]{3,2,1,0:T(8,128)} copy(f32[16,24,24,24]{1,3,2,0:T(8,128)} %convolution_bitcast_fusion) | data formatting | bytes 1769472 | tf_op jit(solution)/shard_map/transpose | solution.py:112
  229.2 22.1 %broadcast_multiply_fusion = f32[13,16,24,24,24]{4,3,2,1,0:T(8,128)} fusion(f32[13,24,24,24]{3,2,1,0:T(8,128)} %maximum_bitcast_fusion, f32[16,24,24,24]{3,2,1,0:T(8,128)} %copy.120), kind=kLoop, calls=%fused_computation.5 | loop fusion | flops 2875392 | bytes 13105152 | tf_op jit(solution)/shard_map/mul | solution.py:125
  251.3 110.7 %fusion.12 = f32[208,24,24,24]{0,1,3,2:T(8,128)} fusion(f32[208,24,24,24]{3,2,1,0:T(8,128)} %bitcast.114, f32[24]{0:T(128)S(1)} %iota_multiply_fusion), kind=kOutput, calls=%fused_computation.12 | convolution fusion | flops 828115200 | bytes 23003232 | tf_op jit(solution)/shard_map/dot_general | solution.py:106
  362.0 21.1 %fusion.6 = f32[208,24,24,24]{0,1,3,2:T(8,128)S(1)} fusion(f32[208,24,24,24]{0,1,3,2:T(8,128)} %fusion.12, f32[24]{0:T(128)S(1)} %iota_multiply_fusion), kind=kOutput, calls=%fused_computation.10 | convolution fusion | flops 828115200 | bytes 23003232 | tf_op jit(solution)/shard_map/dot_general | solution.py:106
  383.2 19.9 %fusion.9 = f32[208,24,24,24]{0,1,3,2:T(8,128)} fusion(f32[208,24,24,24]{0,1,3,2:T(8,128)S(1)} %fusion.6, f32[24]{0:T(128)S(1)} %iota_multiply_fusion), kind=kOutput, calls=%fused_computation.11 | convolution fusion | flops 828115200 | bytes 23003232 | tf_op jit(solution)/shard_map/dot_general | solution.py:106
  403.0 11.8 %slice_multiply_fusion = f32[96,24,24,24]{0,1,3,2:T(8,128)} fusion(f32[208,24,24,24]{0,1,3,2:T(8,128)} %fusion.9), kind=kLoop, calls=%fused_computation.13 | loop fusion | flops 1327104 | bytes 15925248 | tf_op jit(solution)/shard_map/mul | solution.py:129
  414.8 7.7 %slice.449 = f32[16,24,24,24]{0,1,3,2:T(8,128)} slice(f32[208,24,24,24]{0,1,3,2:T(8,128)} %fusion.9), slice={[192:208], [0:24], [0:24], [0:24]} | slice | bytes 1769472 | tf_op jit(solution)/shard_map/slice | solution.py:130
  422.5 9.5 %copy.126 = f32[16,24,24,24]{3,2,1,0:T(8,128)} copy(f32[16,24,24,24]{0,1,3,2:T(8,128)} %slice.449) | data formatting | bytes 1769472 | tf_op jit(solution)/shard_map/slice | solution.py:130
  432.0 5.5 %squeeze.23 = f32[1,16,13824]{2,1,0:T(8,128)} reshape(f32[16,24,24,24]{3,2,1,0:T(8,128)} %copy.126) | data formatting | bytes 1769472 | tf_op jit(solution)/shard_map/squeeze | solution.py:130
  437.5 23.0 %copy.124 = f32[96,24,24,24]{3,2,1,0:T(8,128)} copy(f32[96,24,24,24]{0,1,3,2:T(8,128)} %slice_multiply_fusion) | data formatting | bytes 10616832 | tf_op jit(solution)/shard_map/mul | solution.py:129
  460.5 13.0 %reduce_sum.31 = f32[16,24,24,24]{3,2,1,0:T(8,128)} reduce(f32[6,16,24,24,24]{4,3,2,1,0:T(8,128)} %bitcast.118, f32[]{:T(128)} %constant.144.clone.1), dimensions={0}, to_apply=%region_6.7 | reduce | flops 1105920 | bytes 6193156 | tf_op jit(solution)/shard_map/reduce_sum | solution.py:129
  473.6 5.4 %reduce_sum.32 = f32[1,16,13824]{2,1,0:T(8,128)} reshape(f32[16,24,24,24]{3,2,1,0:T(8,128)} %reduce_sum.31) | data formatting | bytes 1769472 | tf_op jit(solution)/shard_map/reduce_sum | solution.py:129
  479.0 1.6 multiply_subtract_fusion.8
  486.1 3.6 all-to-all-start.1
  490.3 16.8 %all-to-all-done.1 = f32[8,1,16,1728]{3,2,1,0:T(8,128)S(1)} async-done(((f32[8,1,16,1728]{3,2,1,0:T(8,128)}), f32[8,1,16,1728]{3,2,1,0:T(8,128)S(1)}, u32[]{:S(2)}, u32[]{:S(2)}) %all-to-all-start.1) | async-done | bytes 884768 | tf_op jit(solution)/shard_map/all_to_all | solution.py:200
  508.1 3.3 scatter_fusion
  511.5 1.7 copy.127
  (111 shorter events, 35.2 us)
Async XLA Ops:
  4.2 11.9 %copy-start.20 = (s32[1,4]{1,0:T(1,128)S(1)}, s32[1,4]{1,0:T(1,128)}, u32[]{:S(2)}) copy-start(s32[1,4]{1,0:T(1,128)} %param.8) | copy-start | bytes 52
  9.2 20.1 %collective-permute-start.1 = (f32[1,331776]{1,0:T(1,128)S(1)}, f32[1,331776]{1,0:T(1,128)}, u32[]{:S(2)}, u32[]{:S(2)}) collective-permute-start(f32[1,331776]{1,0:T(1,128)S(1)} %constant_dynamic-update-slice_fusion), channel_id=1, source_target_pairs={{8,0},{16,8},{24,16},{9,1},{17,9},{25,17},{10,2},{18,10},{26,18},{... | collective-permute-start | bytes 3981320 | tf_op jit(solution)/shard_map/ppermute | solution.py:23
  11.1 19.2 %collective-permute-start = (f32[1,331776]{1,0:T(1,128)S(1)}, f32[1,331776]{1,0:T(1,128)}, u32[]{:S(2)}, u32[]{:S(2)}) collective-permute-start(f32[1,331776]{1,0:T(1,128)S(1)} %constant_dynamic-update-slice_fusion), channel_id=1, source_target_pairs={{0,8},{8,16},{16,24},{1,9},{9,17},{17,25},{2,10},{10,18},{18,26},{... | collective-permute-start | bytes 3981320 | tf_op jit(solution)/shard_map/ppermute | solution.py:21
  25.0 51.3 %copy-start.10 = (f32[1728]{0:T(1024)}, f32[1728]{0:T(1024)S(1)}, u32[]{:S(2)}) copy-start(f32[1728]{0:T(1024)S(1)} %broadcast_minimum_fusion.1) | copy-start | bytes 20740
  25.0 51.3 %copy-start.12 = (f32[1728]{0:T(1024)}, f32[1728]{0:T(1024)S(1)}, u32[]{:S(2)}) copy-start(f32[1728]{0:T(1024)S(1)} %broadcast_minimum_fusion) | copy-start | bytes 20740
  25.1 51.3 %copy-start.14 = (f32[1728]{0:T(1024)}, f32[1728]{0:T(1024)S(1)}, u32[]{:S(2)}) copy-start(f32[1728]{0:T(1024)S(1)} %broadcast_maximum_fusion) | copy-start | bytes 20740
  25.1 51.3 %copy-start.16 = (f32[1728]{0:T(1024)}, f32[1728]{0:T(1024)S(1)}, u32[]{:S(2)}) copy-start(f32[1728]{0:T(1024)S(1)} %broadcast_maximum_fusion.1) | copy-start | bytes 20740
  53.0 1.2 copy-start.4
  54.4 8.8 %copy-start.5 = (f32[1,3,16,1728]{3,1,2,0:T(4,128)S(1)}, f32[1,3,16,1728]{3,1,2,0:T(4,128)}, u32[]{:S(2)}) copy-start(f32[1,3,16,1728]{3,1,2,0:T(4,128)} %copy.94) | copy-start | bytes 995332
  78.6 1.3 copy-start
  83.2 5.4 %copy-start.8 = (f32[1,82944]{1,0:T(1,128)S(1)}, f32[1,82944]{1,0:T(1,128)}, u32[]{:S(2)}) copy-start(f32[1,82944]{1,0:T(1,128)} %reshape.412) | copy-start | bytes 995332
  84.3 10.7 %copy-start.19 = (s32[256]{0:T(256)S(1)}, s32[256]{0:T(256)}, u32[]{:S(2)}) copy-start(s32[256]{0:T(256)} %param.10) | copy-start | bytes 3076
  88.6 20.1 %collective-permute-start.3 = (f32[1,331776]{1,0:T(1,128)S(1)}, f32[1,331776]{1,0:T(1,128)}, u32[]{:S(2)}, u32[]{:S(2)}) collective-permute-start(f32[1,331776]{1,0:T(1,128)S(1)} %constant_dynamic-update-slice_fusion.7), channel_id=1, source_target_pairs={{8,0},{16,8},{24,16},{9,1},{17,9},{25,17},{10,2},{18,10},{26,18},{... | collective-permute-start | bytes 3981320 | tf_op jit(solution)/shard_map/ppermute | solution.py:23
  90.5 19.2 %collective-permute-start.2 = (f32[1,331776]{1,0:T(1,128)S(1)}, f32[1,331776]{1,0:T(1,128)}, u32[]{:S(2)}, u32[]{:S(2)}) collective-permute-start(f32[1,331776]{1,0:T(1,128)S(1)} %constant_dynamic-update-slice_fusion.7), channel_id=1, source_target_pairs={{0,8},{8,16},{16,24},{1,9},{9,17},{17,25},{2,10},{10,18},{18,26},{... | collective-permute-start | bytes 3981320 | tf_op jit(solution)/shard_map/ppermute | solution.py:21
  132.0 15.2 %copy-start.1 = (f32[1,16,16,1728]{3,1,2,0:T(8,128)S(1)}, f32[1,16,16,1728]{3,1,2,0:T(8,128)}, u32[]{:S(2)}) copy-start(f32[1,16,16,1728]{3,1,2,0:T(8,128)} %copy-done) | copy-start | bytes 5308420
  132.0 15.2 %copy-start.6 = (f32[1,3,16,1728]{3,1,2,0:T(4,128)S(1)}, f32[1,3,16,1728]{3,1,2,0:T(4,128)}, u32[]{:S(2)}) copy-start(f32[1,3,16,1728]{3,1,2,0:T(4,128)} %copy.108) | copy-start | bytes 995332
  132.0 15.2 %copy-start.7 = (f32[1,3,16,1728]{3,1,2,0:T(4,128)S(1)}, f32[1,3,16,1728]{3,1,2,0:T(4,128)}, u32[]{:S(2)}) copy-start(f32[1,3,16,1728]{3,1,2,0:T(4,128)} %copy.107) | copy-start | bytes 995332
  147.3 13.9 %copy-start.11 = (f32[1728]{0:T(1024)S(1)}, f32[1728]{0:T(1024)}, u32[]{:S(2)}) copy-start(f32[1728]{0:T(1024)} %copy-done.10) | copy-start | bytes 20740
  147.3 13.9 %copy-start.13 = (f32[1728]{0:T(1024)S(1)}, f32[1728]{0:T(1024)}, u32[]{:S(2)}) copy-start(f32[1728]{0:T(1024)} %copy-done.12) | copy-start | bytes 20740
  147.3 13.9 %copy-start.15 = (f32[1728]{0:T(1024)S(1)}, f32[1728]{0:T(1024)}, u32[]{:S(2)}) copy-start(f32[1728]{0:T(1024)} %copy-done.14) | copy-start | bytes 20740
  147.3 13.9 %copy-start.17 = (f32[1728]{0:T(1024)S(1)}, f32[1728]{0:T(1024)}, u32[]{:S(2)}) copy-start(f32[1728]{0:T(1024)} %copy-done.16) | copy-start | bytes 20740
  166.2 6.6 %copy-start.18 = (f32[13824]{0:T(1024)S(1)}, f32[13824]{0:T(1024)}, u32[]{:S(2)}) copy-start(f32[13824]{0:T(1024)} %param.13) | copy-start | bytes 165892
  166.2 6.8 %copy-start.9 = (f32[6,13824]{1,0:T(8,128)S(1)}, f32[6,13824]{1,0:T(8,128)}, u32[]{:S(2)}) copy-start(f32[6,13824]{1,0:T(8,128)} %param.11) | copy-start | bytes 995332
  167.3 19.4 %all-to-all-start = ((f32[8,16,1728]{2,1,0:T(8,128)}), f32[8,16,1728]{2,1,0:T(8,128)S(1)}, u32[]{:S(2)}, u32[]{:S(2)}) async-start(f32[8,16,1728]{2,1,0:T(8,128)} %broadcast_multiply_fusion.1), calls=%async_computation | async-start | bytes 1835008 | tf_op jit(solution)/shard_map/all_to_all | solution.py:184
  186.7 0.9 copy-start.2
  473.6 5.4 %copy-start.3 = (f32[1,16,13824]{2,1,0:T(8,128)S(1)}, f32[1,16,13824]{2,1,0:T(8,128)}, u32[]{:S(2)}) copy-start(f32[1,16,13824]{2,1,0:T(8,128)} %reshape_squeeze.3) | copy-start | bytes 2654212
  486.1 21.0 %all-to-all-start.1 = ((f32[8,1,16,1728]{3,2,1,0:T(8,128)}), f32[8,1,16,1728]{3,2,1,0:T(8,128)S(1)}, u32[]{:S(2)}, u32[]{:S(2)}) async-start(f32[8,1,16,1728]{3,2,1,0:T(8,128)} %fusion.151), calls=%async_computation.1 | async-start | bytes 1835008 | tf_op jit(solution)/shard_map/all_to_all | solution.py:200
